TPU v7x, 128 devices: a whole 4x4x4 slice. The times are simulated.
128 devices in a mesh: layer: 4 (over y_lo, core), latent: 16 (over x, z), row: 2 (over y_hi).
Axes of the slice: x: 4, y: 4 (y_hi: 2, y_lo: 2; y = y_hi * 2 + y_lo), z: 4, core: 2. Of those that a mesh axis runs over, the one named last changes fastest.
Arguments:
- inputs: bfloat16 [1024, 4, 3584], P('row', 'layer'), may hold values from -6 to 6
- clean_acts: bfloat16 [1024, 4, 3584], P('row', 'layer'), may hold values from -6 to 6
- enc_weight: bfloat16 [4, 3584, 12288], P('layer', None, 'latent'), may hold values from -0.0625 to 0.0625
- enc_bias: float32 [12288], P('latent'), may hold values from -3 to 3
- dec_weight: bfloat16 [4, 12288, 3584], P('layer', 'latent'), may hold values from -0.109375 to 0.109375
- dec_bias: float32 [4, 3584], P('layer'), may hold values from -3 to 3
- pairing: int32 [1024], replicated, may hold values from 0 to 1023, each once
- targets: int32 [1024], replicated, may hold values from 0 to 12287
Outputs:
- input_grad: bfloat16 [1024, 4, 3584], P('row', 'layer', 'latent')
Inputs may be any that keep to these rules, and one draw needn't show every extreme that they name: pairing is a permutation of the rows.
All inputs are finite; a program needn't handle non-finite values.
Results may differ from a plain program's by a relative error of at most 0.018.
Values may be sent and summed in bfloat16 or wider, within the bound.
A program may use at most 128 MiB of HBM per device.

v0:
```python
import jax
import jax.numpy as jnp
from jax import lax
from jax.sharding import PartitionSpec as P

MARGIN = 16.0


def local(inputs, clean_acts, enc_weight, enc_bias, dec_weight, dec_bias, pairing, targets):
    row_count = inputs.shape[0]
    lat_count = enc_weight.shape[2]
    all_rows = pairing.shape[0]
    partial_pre = jnp.einsum("rld,ldf->rf", inputs, enc_weight, preferred_element_type=jnp.float32)
    preact = lax.psum(partial_pre, "layer") + enc_bias
    features = jnp.maximum(preact, 0.0).astype(jnp.bfloat16)
    partial_recon = jnp.einsum(
        "rf,lfd->rld", features, dec_weight, preferred_element_type=jnp.float32
    )
    recon = (
        lax.psum(partial_recon.astype(jnp.bfloat16), "latent").astype(jnp.float32) + dec_bias[None]
    )
    recon_error = (recon - clean_acts.astype(jnp.float32)).astype(jnp.bfloat16)
    partial_grad = jnp.einsum(
        "rld,lfd->rf", recon_error, dec_weight, preferred_element_type=jnp.float32
    )
    feat_grad = lax.psum(partial_grad.astype(jnp.bfloat16), "layer").astype(jnp.float32)
    row_ids = lax.axis_index("row") * row_count + jnp.arange(row_count, dtype=jnp.int32)
    latent_ids = lax.axis_index("latent") * lat_count + jnp.arange(lat_count, dtype=jnp.int32)
    every_row = jnp.arange(all_rows, dtype=jnp.int32)
    pair_table = (
        (every_row[None, :] == row_ids[:, None]).astype(jnp.float32)
        - (pairing[None, :] == row_ids[:, None]).astype(jnp.float32)
    ).astype(jnp.bfloat16)
    target_hot = (targets[:, None] == latent_ids[None, :]).astype(jnp.bfloat16)
    margin_table = jnp.dot(pair_table, target_hot, preferred_element_type=jnp.float32)
    pre_grad = jnp.where(preact > 0, feat_grad - MARGIN * margin_table, 0.0).astype(jnp.bfloat16)
    partial_input = jnp.einsum(
        "rf,ldf->rld", pre_grad, enc_weight, preferred_element_type=jnp.float32
    )
    return lax.psum_scatter(
        partial_input.astype(jnp.bfloat16), "latent", scatter_dimension=2, tiled=True
    )


def solution(mesh):
    placed = (
        P("row", "layer", None),
        P("row", "layer", None),
        P("layer", None, "latent"),
        P("latent"),
        P("layer", "latent", None),
        P("layer", None),
        P(),
        P(),
    )
    return jax.shard_map(
        local, mesh=mesh, in_specs=placed, out_specs=P("row", "layer", "latent"), check_vma=False
    )
```

profile of v0, /device:TPU:0, one launch (start us, length us, event | category | flops | bytes accessed | tf_op | source)
XLA Modules:
  0.0 339.5 jit_solution(3582329185027810856)
XLA Ops:
  6.5 7.9 %fusion.4 = f32[512,768]{1,0:T(8,128)} fusion(bf16[1,3584,768]{2,1,0:T(8,128)(2,1)} %param.10, bf16[512,1,3584]{2,0,1:T(8,128)(2,1)} %param.8), kind=kOutput, calls=%fused_computation.7 | convolution fusion | flops 2818572288 | bytes 10747904 | tf_op jit(solution)/shard_map/rld,ldf->rf/dot_general | solution.py:13
  14.4 0.0 all-reduce.4.cloned.1.call-update
  14.4 0.0 all-reduce.6.cloned.1.call-start
  14.5 51.4 %all-reduce.4.cloned.1.call-done = f32[512,768]{1,0:T(8,128)} async-done(((f32[512,768]{1,0:T(8,128)}), f32[512,768]{1,0:T(8,128)}) %all-reduce.4.cloned.1.call-update) | async-done | bytes 1572880 | tf_op jit(solution)/shard_map/psum | solution.py:14
  65.8 0.0 copy-done.2
  65.8 7.9 %fusion.6 = bf16[512,1,3584]{2,0,1:T(8,128)(2,1)} fusion(bf16[1,768,3584]{2,1,0:T(8,128)(2,1)} %param.12, f32[512,768]{1,0:T(8,128)} %all-reduce.4.cloned.1.call-done, f32[768]{0:T(1024)S(1)} %copy-done.2), kind=kOutput, calls=%fused_computation.9 | convolution fusion | flops 2821586944 | bytes 10750976 | tf_op jit(solution)/shard_map/rf,lfd->rld/dot_general | solution.py:16
  73.8 0.0 all-reduce.6.cloned.1.call-update
  73.8 0.0 all-reduce.8.cloned.1.call-start
  73.8 0.6 copy-done
  74.5 0.0 copy-start.3
  74.5 0.0 copy-start.4
  74.5 99.5 %all-reduce.6.cloned.1.call-done = bf16[512,1,3584]{2,0,1:T(8,128)(2,1)} async-done(((bf16[512,1,3584]{2,0,1:T(8,128)(2,1)}), bf16[512,1,3584]{2,0,1:T(8,128)(2,1)}) %all-reduce.6.cloned.1.call-update) | async-done | bytes 3670032 | tf_op jit(solution)/shard_map/psum | solution.py:20
  174.0 8.8 %fusion.20 = bf16[512,768]{1,0:T(8,128)(2,1)} fusion(bf16[1,768,3584]{2,1,0:T(8,128)(2,1)} %param.12, bf16[512,1,3584]{2,0,1:T(8,128)(2,1)} %param.9, bf16[512,1,3584]{2,0,1:T(8,128)(2,1)} %all-reduce.6.cloned.1.call-done, f32[3584]{0:T(1024)S(1)} %reduce), kind=kOutput, calls=%fused_computation.23 | convolution fusion | flops 2828140544 | bytes 13645824 | tf_op jit(solution)/shard_map/rld,lfd->rf/dot_general | solution.py:23
  182.7 0.0 all-reduce.8.cloned.1.call-update
  182.8 0.2 reduce-scatter.4.cloned.1.call-start
  183.0 38.4 %all-reduce.8.cloned.1.call-done = bf16[512,768]{1,0:T(8,128)(2,1)} async-done(((bf16[512,768]{1,0:T(8,128)(2,1)}), bf16[512,768]{1,0:T(8,128)(2,1)}) %all-reduce.8.cloned.1.call-update) | async-done | bytes 786448 | tf_op jit(solution)/shard_map/psum | solution.py:26
  221.4 0.0 copy-done.3
  221.4 9.4 %fusion.9 = bf16[512,1,3584]{2,0,1:T(8,128)(2,1)} fusion(bf16[1,3584,768]{2,1,0:T(8,128)(2,1)} %param.10, bf16[512,768]{1,0:T(8,128)(2,1)} %all-reduce.8.cloned.1.call-done, f32[512,768]{1,0:T(8,128)S(1)} %copy-done.1, s32[768]{0:T(1024)S(1)} %iota_add_fusion, s32[1024]{0:T(1024)S(1)} %copy-done.3, s32[1024]{0:T(1024)S(1)} %copy-done.4, ...), kind=kOutput, calls=%fused_computation.10 | convolution fusion | flops 3632398336 | bytes 11550720 | tf_op jit(solution)/shard_map/rf,ldf->rld/dot_general | solution.py:37
  230.8 16.5 %copy.11 = bf16[512,1,3584]{0,1,2:T(2,128)(2,1)} copy(bf16[512,1,3584]{2,0,1:T(8,128)(2,1)} %fusion.9) | data formatting | bytes 7340032
  247.3 6.1 %copy.16 = bf16[3584,1,512]{2,0,1:T(8,128)(2,1)} copy(bf16[3584,1,512]{2,1,0:T(2,128)(2,1)} %bitcast.35) | data formatting | bytes 7340032
  253.4 0.0 reduce-scatter.4.cloned.1.call-update
  253.4 77.7 %reduce-scatter.4.cloned.1.call-done = bf16[224,512]{1,0:T(8,128)(2,1)} async-done(((bf16[3584,512]{1,0:T(8,128)(2,1)}), bf16[224,512]{1,0:T(8,128)(2,1)}) %reduce-scatter.4.cloned.1.call-update) | async-done | bytes 229392
  331.1 1.2 reshape_bitcast_fusion
  332.3 0.7 copy.10
  (9 shorter events, 0.1 us)
Async XLA Ops:
  6.5 59.3 %copy-start.2 = (f32[768]{0:T(1024)S(1)}, f32[768]{0:T(1024)}, u32[]{:S(2)}) copy-start(f32[768]{0:T(1024)} %param.11) | copy-start | bytes 9220
  6.5 59.3 %all-reduce.4.cloned.1.call-start = ((), (), s32[]{:S(2)}) async-start(), calls=%async_computation.1 | async-start | bytes 3145728 | tf_op jit(solution)/shard_map/psum | solution.py:14
  14.4 159.6 %all-reduce.6.cloned.1.call-start = ((), (), s32[]{:S(2)}) async-start(), calls=%async_computation.2 | async-start | bytes 7340032 | tf_op jit(solution)/shard_map/psum | solution.py:20
  73.8 0.7 copy-start
  73.8 147.6 %all-reduce.8.cloned.1.call-start = ((), (), s32[]{:S(2)}) async-start(), calls=%async_computation.3 | async-start | bytes 1572864 | tf_op jit(solution)/shard_map/psum | solution.py:26
  74.5 146.9 %copy-start.1 = (f32[512,768]{1,0:T(8,128)S(1)}, f32[512,768]{1,0:T(8,128)}, u32[]{:S(2)}) copy-start(f32[512,768]{1,0:T(8,128)} %all-reduce.4.cloned.1.call-done) | copy-start | bytes 4718596
  74.5 146.9 %copy-start.3 = (s32[1024]{0:T(1024)S(1)}, s32[1024]{0:T(1024)}, u32[]{:S(2)}) copy-start(s32[1024]{0:T(1024)} %param.15) | copy-start | bytes 12292
  74.5 146.9 %copy-start.4 = (s32[1024]{0:T(1024)S(1)}, s32[1024]{0:T(1024)}, u32[]{:S(2)}) copy-start(s32[1024]{0:T(1024)} %param.14) | copy-start | bytes 12292
  182.8 148.3 %reduce-scatter.4.cloned.1.call-start = ((), (), s32[]{:S(2)}) async-start(), calls=%async_computation.4 | async-start | bytes 3899392
Sparse Core Ops, SparseCore 0:
  14.5 51.2 all-reduce.3
  73.9 100.0 all-reduce.5
  182.9 38.4 all-reduce.7
  253.5 77.5 reduce-scatter.3
where the time goes:
time: 340 us
  waiting for transfers between devices  267 us (79%)
  matrix products  33.9 us (10%)
  local copies, waits for them, and re-layouts  25.1 us (7%)
  between operations  13.2 us (4%)
    psum x1, waiting for transfers between devices, local(): lax.psum(partial_recon.astype(jnp.bfloat16), 'latent').astype(jnp.float32)  99.5 us
    unnamed x5, waiting for transfers between devices  77.7 us
    psum x1, waiting for transfers between devices, local(): preact = lax.psum(partial_pre, 'layer') + enc_bias  51.4 us
    psum x1, waiting for transfers between devices, local(): lax.psum(partial_grad.astype(jnp.bfloat16), 'layer').astype(jnp.float32)  38.4 us
    unnamed x13, local copies, waits for them, and re-layouts  24.4 us
    dot_general x1, matrix products, local(): jnp.einsum('rf,ldf->rld', pre_grad, enc_weight, preferred_element_type=jn...  9.4 us
    dot_general x1, matrix products, local(): jnp.einsum('rld,lfd->rf', recon_error, dec_weight, preferred_element_type...  8.75 us
    dot_general x1, matrix products, local(): jnp.einsum('rf,lfd->rld', features, dec_weight, preferred_element_type=jn...  7.9 us
  transfers between devices with their start and end apart: 4, of which 4 were waited for; matrix products, arithmetic and copies ran while one was open for 0% of the time, Pallas kernels for 0%

commit v1 on v0

--- a/solution.py
+++ b/solution.py
@@ -17,7 +17,10 @@
         "rf,lfd->rld", features, dec_weight, preferred_element_type=jnp.float32
     )
     recon = (
-        lax.psum(partial_recon.astype(jnp.bfloat16), "latent").astype(jnp.float32) + dec_bias[None]
+        jnp.sum(lax.all_gather(partial_recon.astype(jnp.bfloat16), "latent"), axis=0).astype(
+            jnp.float32
+        )
+        + dec_bias[None]
     )
     recon_error = (recon - clean_acts.astype(jnp.float32)).astype(jnp.bfloat16)
     partial_grad = jnp.einsum(

time: 340 us -> 589 us (1.73)
  waiting for transfers between devices: 267 us -> 494 us
  other arithmetic: 0.04 us -> 21.5 us
    all_gather x0 -> x1, waiting for transfers between devices: none -> 326 us  [local(): lax.all_gather(partial_recon.astype(jnp.bfloat16), 'latent')]
    psum x1 -> x0, waiting for transfers between devices: 99.5 us -> none  [local(): lax.psum(partial_recon.astype(jnp.bfloat16), 'latent').astype(jnp.float32)]
    reduce_sum x0 -> x1, other arithmetic: none -> 21.4 us  [local(): jnp.sum(lax.all_gather(partial_recon.astype(jnp.bfloat16), 'latent'), axi...]
where the time goes in v1:
time: 589 us; the launch traced here: 588 us
  waiting for transfers between devices  494 us (84%)
  matrix products  34.1 us (6%)
  local copies, waits for them, and re-layouts  25.1 us (4%)
  other arithmetic  21.5 us (4%)
  between operations  13.2 us (2%)
    all_gather x1, waiting for transfers between devices, local(): lax.all_gather(partial_recon.astype(jnp.bfloat16), 'latent')  326 us
    unnamed x5, waiting for transfers between devices  77.7 us
    psum x1, waiting for transfers between devices, local(): preact = lax.psum(partial_pre, 'layer') + enc_bias  51.4 us
    psum x1, waiting for transfers between devices, local(): lax.psum(partial_grad.astype(jnp.bfloat16), 'layer').astype(jnp.float32)  38.8 us
    unnamed x13, local copies, waits for them, and re-layouts  24.4 us
    reduce_sum x1, other arithmetic, local(): jnp.sum(lax.all_gather(partial_recon.astype(jnp.bfloat16), 'latent'), axi...  21.4 us
  transfers between devices with their start and end apart: 4, of which 4 were waited for; matrix products, arithmetic and copies ran while one was open for 0% of the time, Pallas kernels for 0%

profile of v1, /device:TPU:0, one launch (start us, length us, event | category | flops | bytes accessed | tf_op | source)
XLA Modules:
  0.0 588.2 jit_solution(13281694161559621516)
XLA Ops:
  6.5 0.0 all-reduce.3.cloned.1.call-start
  6.5 8.0 %fusion.6 = f32[512,768]{1,0:T(8,128)} fusion(bf16[1,3584,768]{2,1,0:T(8,128)(2,1)} %param.10, bf16[512,1,3584]{2,0,1:T(8,128)(2,1)} %param.8), kind=kOutput, calls=%fused_computation.9 | convolution fusion | flops 2818572288 | bytes 10747904 | tf_op jit(solution)/shard_map/rld,ldf->rf/dot_general | solution.py:13
  14.5 0.0 all-reduce.3.cloned.1.call-update
  14.5 0.0 all-gather.3.cloned.1.call-start
  14.6 51.4 %all-reduce.3.cloned.1.call-done = f32[512,768]{1,0:T(8,128)} async-done(((f32[512,768]{1,0:T(8,128)}), f32[512,768]{1,0:T(8,128)}) %all-reduce.3.cloned.1.call-update) | async-done | bytes 1572880 | tf_op jit(solution)/shard_map/psum | solution.py:14
  66.0 0.0 copy-done.2
  66.0 7.8 %convolution_convert_fusion.1 = bf16[512,3584]{1,0:T(8,128)(2,1)} fusion(bf16[1,768,3584]{2,1,0:T(8,128)(2,1)} %param.12, f32[512,768]{1,0:T(8,128)} %all-reduce.3.cloned.1.call-done, f32[768]{0:T(1024)S(1)} %copy-done.2), kind=kOutput, calls=%fused_computation.4 | convolution fusion | flops 2821586944 | bytes 10750976 | tf_op jit(solution)/shard_map/rf,lfd->rld/dot_general | solution.py:16
  73.8 0.0 all-gather.3.cloned.1.call-update
  73.8 0.0 all-reduce.5.cloned.1.call-start
  73.9 0.6 copy-done
  74.5 326.3 %all-gather.3.cloned.1.call-done = bf16[8192,3584]{1,0:T(8,128)(2,1)} async-done(((bf16[512,3584]{1,0:T(8,128)(2,1)}), bf16[8192,3584]{1,0:T(8,128)(2,1)}) %all-gather.3.cloned.1.call-update) | async-done | bytes 58720272 | tf_op jit(solution)/shard_map/all_gather | solution.py:20
  400.8 21.4 %reduce.2 = bf16[512,3584]{1,0:T(8,128)(2,1)} reduce(bf16[16,512,3584]{2,1,0:T(8,128)(2,1)} %bitcast.40, bf16[]{:T(256)} %constant.4.clone.1), dimensions={0}, to_apply=%region_1.0 | reduce | flops 27525120 | bytes 62390272 | tf_op jit(solution)/shard_map/reduce_sum | solution.py:20
  422.2 8.9 %fusion.20 = bf16[512,768]{1,0:T(8,128)(2,1)} fusion(bf16[1,768,3584]{2,1,0:T(8,128)(2,1)} %param.12, bf16[512,1,3584]{2,0,1:T(8,128)(2,1)} %param.9, bf16[512,3584]{1,0:T(8,128)(2,1)} %reduce.2, f32[3584]{0:T(1024)S(1)} %reduce.3), kind=kOutput, calls=%fused_computation.25 | convolution fusion | flops 2828140544 | bytes 13645824 | tf_op jit(solution)/shard_map/rld,lfd->rf/dot_general | solution.py:26
  431.1 0.0 all-reduce.5.cloned.1.call-update
  431.1 0.2 reduce-scatter.4.cloned.1.call-start
  431.4 38.8 %all-reduce.5.cloned.1.call-done = bf16[512,768]{1,0:T(8,128)(2,1)} async-done(((bf16[512,768]{1,0:T(8,128)(2,1)}), bf16[512,768]{1,0:T(8,128)(2,1)}) %all-reduce.5.cloned.1.call-update) | async-done | bytes 786448 | tf_op jit(solution)/shard_map/psum | solution.py:29
  470.2 0.0 copy-done.4
  470.2 9.4 %fusion.8 = bf16[512,1,3584]{2,0,1:T(8,128)(2,1)} fusion(bf16[1,3584,768]{2,1,0:T(8,128)(2,1)} %param.10, bf16[512,768]{1,0:T(8,128)(2,1)} %all-reduce.5.cloned.1.call-done, f32[512,768]{1,0:T(8,128)S(1)} %copy-done.1, s32[768]{0:T(1024)S(1)} %iota_add_fusion, s32[1024]{0:T(1024)S(1)} %copy-done.3, s32[1024]{0:T(1024)S(1)} %copy-done.4, ...), kind=kOutput, calls=%fused_computation.11 | convolution fusion | flops 3632398336 | bytes 11550720 | tf_op jit(solution)/shard_map/rf,ldf->rld/dot_general | solution.py:40
  479.6 16.5 %copy.11 = bf16[512,1,3584]{0,1,2:T(2,128)(2,1)} copy(bf16[512,1,3584]{2,0,1:T(8,128)(2,1)} %fusion.8) | data formatting | bytes 7340032
  496.1 6.1 %copy.16 = bf16[3584,1,512]{2,0,1:T(8,128)(2,1)} copy(bf16[3584,1,512]{2,1,0:T(2,128)(2,1)} %bitcast.41) | data formatting | bytes 7340032
  502.2 0.0 reduce-scatter.4.cloned.1.call-update
  502.2 77.6 %reduce-scatter.4.cloned.1.call-done = bf16[224,512]{1,0:T(8,128)(2,1)} async-done(((bf16[3584,512]{1,0:T(8,128)(2,1)}), bf16[224,512]{1,0:T(8,128)(2,1)}) %reduce-scatter.4.cloned.1.call-update) | async-done | bytes 229392
  579.8 1.2 reshape_bitcast_fusion
  581.0 0.7 copy.10
  (10 shorter events, 0.1 us)
Async XLA Ops:
  6.5 59.4 %copy-start.2 = (f32[768]{0:T(1024)S(1)}, f32[768]{0:T(1024)}, u32[]{:S(2)}) copy-start(f32[768]{0:T(1024)} %param.11) | copy-start | bytes 9220
  6.5 59.4 %all-reduce.3.cloned.1.call-start = ((), (), s32[]{:S(2)}) async-start(), calls=%async_computation.1 | async-start | bytes 3145728 | tf_op jit(solution)/shard_map/psum | solution.py:14
  14.5 386.3 %all-gather.3.cloned.1.call-start = ((), (), s32[]{:S(2)}) async-start(), calls=%async_computation.3 | async-start | bytes 62390272 | tf_op jit(solution)/shard_map/all_gather | solution.py:20
  73.8 0.7 copy-start
  73.8 396.3 %all-reduce.5.cloned.1.call-start = ((), (), s32[]{:S(2)}) async-start(), calls=%async_computation.2 | async-start | bytes 1572864 | tf_op jit(solution)/shard_map/psum | solution.py:29
  422.2 47.9 %copy-start.1 = (f32[512,768]{1,0:T(8,128)S(1)}, f32[512,768]{1,0:T(8,128)}, u32[]{:S(2)}) copy-start(f32[512,768]{1,0:T(8,128)} %all-reduce.3.cloned.1.call-done) | copy-start | bytes 4718596
  422.2 47.9 %copy-start.3 = (s32[1024]{0:T(1024)S(1)}, s32[1024]{0:T(1024)}, u32[]{:S(2)}) copy-start(s32[1024]{0:T(1024)} %param.15) | copy-start | bytes 12292
  422.2 47.9 %copy-start.4 = (s32[1024]{0:T(1024)S(1)}, s32[1024]{0:T(1024)}, u32[]{:S(2)}) copy-start(s32[1024]{0:T(1024)} %param.14) | copy-start | bytes 12292
  431.1 148.6 %reduce-scatter.4.cloned.1.call-start = ((), (), s32[]{:S(2)}) async-start(), calls=%async_computation.4 | async-start | bytes 3899392
Sparse Core Ops, SparseCore 0:
  14.7 51.2 all-reduce.2
  73.9 326.8 all-gather.2
  431.3 38.8 all-reduce.4
  502.3 77.4 reduce-scatter.3
